TPU v7x, 128 devices: a whole 4x4x4 slice. The times are simulated.
128 devices in a mesh: wide: 32 (over x, z, core), narrow: 4 (over y).
Axes of the slice: x: 4, y: 4, z: 4, core: 2. Of those that a mesh axis runs over, the one named last changes fastest.
Arguments:
- front: bfloat16 [4, 32, 128, 32, 4, 128], P(None, 'wide', None, None, 'narrow'), may hold values from -6 to 6
- pivot_inverse: bfloat16 [4, 128, 128], replicated, may hold values from -0.0105112052 to 0.17838107
- rhs: bfloat16 [4, 32, 128, 256], P(None, 'wide'), may hold values from -6 to 6
- trail_sol: bfloat16 [4, 32, 128, 256], P(None, 'wide'), may hold values from -1.1953125 to 1.1953125
- block_mask: int32 [4, 32, 32, 4], P(None, 'wide', None, 'narrow'), may hold values 0 or 1
- panel_order: int32 [4], replicated, may hold values from 0 to 3, each once
Outputs:
- front_out: bfloat16 [4, 32, 128, 32, 4, 128], P(None, 'wide', None, None, 'narrow')
- forward_rhs: bfloat16 [4, 32, 128, 256], P(None, 'wide')
- window_solution: bfloat16 [4, 128, 256], replicated
Inputs may be any that keep to these rules, and one draw needn't show every extreme that they name: `panel_order`: each value 0 to 3 appears once.
All inputs are finite; a program needn't handle non-finite values. No bound on the sum of `block_mask` on one device may be relied on, other than what follows from the above.
Results may differ from a plain program's by a relative error of at most 0.0076.
Values may be sent and summed in bfloat16 or wider, within the bound.
No kernel may reach another device: no remote copies, remote signals or barrier semaphores. Data moves between devices by JAX's collectives and lax.ppermute only.
A program may use at most 64 MiB of HBM per device.

v0:
```python
import jax
import jax.numpy as jnp
from jax import lax
from jax.sharding import PartitionSpec as P


def spread(block, axis, source):
    block = jnp.where(lax.axis_index(axis) == source, block, jnp.zeros_like(block))
    return lax.psum(block, axis)


def body(front, pivot_inverse, rhs, trail_sol, block_mask, panel_order):
    rloc = front.shape[0]
    bsize = front.shape[2]
    cloc = front.shape[3]
    nrhs_local = rhs.shape[3]
    panels = panel_order.shape[0]
    nwide = lax.axis_size("wide")
    nnarrow = lax.axis_size("narrow")
    blocks = front.reshape(rloc, bsize, cloc, bsize)
    pattern = block_mask.reshape(rloc, cloc).astype(jnp.float32)
    right = rhs.reshape(rloc, bsize, nrhs_local)
    rows_global = jnp.arange(rloc, dtype=jnp.int32) * nwide + lax.axis_index("wide")
    cols_global = jnp.arange(cloc, dtype=jnp.int32) * nnarrow + lax.axis_index("narrow")
    section_ids = jnp.arange(panels, dtype=jnp.int32)
    rows_rank = jnp.min(
        jnp.where(rows_global[:, None] == panel_order[None, :], section_ids[None, :], panels),
        axis=1,
    )
    cols_rank = jnp.min(
        jnp.where(cols_global[:, None] == panel_order[None, :], section_ids[None, :], panels),
        axis=1,
    )

    def pivot_weight(target):
        return lax.dynamic_index_in_dim(pivot_inverse, target, 0, keepdims=False)

    def panel_factors(col_blocks, row_blocks, target, section):
        weight = pivot_weight(target)
        left = jnp.einsum("rab,bc->rac", col_blocks, weight, preferred_element_type=jnp.float32)
        left = jnp.where((rows_rank > section)[:, None, None], left, 0.0).astype(jnp.bfloat16)
        left = spread(left, "narrow", target % nnarrow)
        upper = jnp.einsum("ac,ajb->cjb", weight, row_blocks, preferred_element_type=jnp.float32)
        upper = jnp.where((cols_rank > section)[None, :, None], upper, 0.0).astype(jnp.bfloat16)
        upper = spread(upper, "wide", target % nwide)
        return (left, upper)

    def column_of(current, target):
        return lax.dynamic_index_in_dim(current, target // nnarrow, 2, keepdims=False)

    def row_of(current, target):
        return lax.dynamic_index_in_dim(current, target // nwide, 0, keepdims=False)

    saved_left = []
    saved_pivot = []
    left, upper = panel_factors(
        column_of(blocks, panel_order[0]), row_of(blocks, panel_order[0]), panel_order[0], 0
    )
    for section in range(panels):
        target = panel_order[section]
        weight = pivot_weight(target)
        product = jnp.einsum("rac,cjb->rajb", left, upper, preferred_element_type=jnp.float32)
        blocks = (blocks.astype(jnp.float32) - pattern[:, None, :, None] * product).astype(
            jnp.bfloat16
        )
        if section + 1 < panels:
            following = panel_order[section + 1]
            next_left, next_upper = panel_factors(
                column_of(blocks, following), row_of(blocks, following), following, section + 1
            )
        pivot_rhs = lax.dynamic_index_in_dim(right, target // nwide, 0, keepdims=False)
        solved = jnp.einsum(
            "ac,an->cn", weight, pivot_rhs, preferred_element_type=jnp.float32
        ).astype(jnp.bfloat16)
        solved = spread(solved, "wide", target % nwide)
        elimination = jnp.einsum("rac,cn->ran", left, solved, preferred_element_type=jnp.float32)
        right = (right.astype(jnp.float32) - elimination).astype(jnp.bfloat16)
        saved_left.append(left)
        saved_pivot.append(solved)
        if section + 1 < panels:
            left, upper = (next_left, next_upper)
    current = trail_sol.reshape(rloc, bsize, nrhs_local)
    window = jnp.zeros((panels, bsize, nrhs_local), jnp.bfloat16)
    for section in reversed(range(panels)):
        target = panel_order[section]
        partial_sum = jnp.einsum(
            "rac,ran->cn", saved_left[section], current, preferred_element_type=jnp.float32
        )
        total = lax.psum(partial_sum, "wide")
        corrected = (saved_pivot[section].astype(jnp.float32) - total).astype(jnp.bfloat16)
        result = jnp.einsum(
            "ac,cn->an", pivot_weight(target), corrected, preferred_element_type=jnp.float32
        ).astype(jnp.bfloat16)
        current = jnp.where((rows_global == target)[:, None, None], result[None], current)
        window = lax.dynamic_update_index_in_dim(window, result, target, 0)
    return (blocks.reshape(front.shape), right.reshape(rhs.shape), window)


def solution(mesh):
    in_specs = (
        P(None, "wide", None, None, "narrow", None),
        P(),
        P(None, "wide", None, None),
        P(None, "wide", None, None),
        P(None, "wide", None, "narrow"),
        P(),
    )
    out_specs = (P(None, "wide", None, None, "narrow", None), P(None, "wide", None, None), P())
    return jax.shard_map(body, mesh=mesh, in_specs=in_specs, out_specs=out_specs, check_vma=False)
```

profile of v0, /device:TPU:1, one launch (start us, length us, event | category | flops | bytes accessed | tf_op | source)
XLA Modules:
  0.0 1070.7 jit_solution(9461470469571352421)
XLA Ops:
  7.2 1.5 fusion.111
  12.6 0.8 select_reduce_fusion.1
  13.5 1.5 constant_dynamic-slice_fusion.1
  15.0 0.8 fusion.18
  15.9 0.0 all-reduce.39.cloned.1.call-start
  16.0 1.3 constant_dynamic-slice_fusion
  17.3 0.7 select_reduce_fusion
  18.1 1.6 fusion.2
  19.7 0.8 fusion.19
  20.5 0.0 all-reduce.19.cloned.1.call-start
  24.1 34.5 %all-reduce.17.cloned.1.call-done = bf16[4,128,128]{2,1,0:T(8,128)(2,1)} async-done(((bf16[4,128,128]{2,1,0:T(8,128)(2,1)}), bf16[4,128,128]{2,1,0:T(8,128)(2,1)}) %all-reduce.17.cloned.1.call-update) | async-done | bytes 131088 | tf_op jit(solution)/shard_map/psum | solution.py:9
  58.6 112.0 %all-reduce.39.cloned.1.call-done = (bf16[128,32,128]{2,0,1:T(8,128)(2,1)}, bf16[128,256]{1,0:T(8,128)(2,1)}) async-done(((bf16[128,32,128]{2,0,1:T(8,128)(2,1)}, bf16[128,256]{1,0:T(8,128)(2,1)}), (bf16[128,32,128]{2,0,1:T(8,128)(2,1)}, bf16[128,256]{1,0:T(8,128)(2,1)})) %all-reduce.39.cloned.1.call-update) | async-done | bytes 1114128 | tf_op jit(solution)/shard_map/psum | solution.py:9
  170.6 4.7 fusion
  175.3 2.0 copy-done.2
  177.3 0.8 fusion.17
  178.2 0.0 all-reduce.37.cloned.1.call-start
  178.2 2.7 fusion.3
  180.9 0.2 fusion.6
  181.1 0.8 fusion.20
  182.0 0.0 all-reduce.21.cloned.1.call-start
  185.6 31.7 %all-reduce.19.cloned.1.call-done = bf16[4,128,128]{2,1,0:T(8,128)(2,1)} async-done(((bf16[4,128,128]{2,1,0:T(8,128)(2,1)}), bf16[4,128,128]{2,1,0:T(8,128)(2,1)}) %all-reduce.19.cloned.1.call-update) | async-done | bytes 131088 | tf_op jit(solution)/shard_map/psum | solution.py:9
  217.3 111.8 %all-reduce.37.cloned.1.call-done = (bf16[128,32,128]{2,0,1:T(8,128)(2,1)}, bf16[128,256]{1,0:T(8,128)(2,1)}) async-done(((bf16[128,32,128]{2,0,1:T(8,128)(2,1)}, bf16[128,256]{1,0:T(8,128)(2,1)}), (bf16[128,32,128]{2,0,1:T(8,128)(2,1)}, bf16[128,256]{1,0:T(8,128)(2,1)})) %all-reduce.37.cloned.1.call-update) | async-done | bytes 1114128 | tf_op jit(solution)/shard_map/psum | solution.py:9
  329.1 3.8 subtract_convert_fusion.2
  333.0 2.0 copy-done.1
  335.0 0.8 fusion.16
  335.8 0.0 all-reduce.35.cloned.1.call-start
  335.9 2.7 fusion.4
  338.6 0.2 fusion.7
  338.8 0.8 fusion.21
  339.6 0.0 all-reduce.23.cloned.1.call-start
  343.9 31.0 %all-reduce.21.cloned.1.call-done = bf16[4,128,128]{2,1,0:T(8,128)(2,1)} async-done(((bf16[4,128,128]{2,1,0:T(8,128)(2,1)}), bf16[4,128,128]{2,1,0:T(8,128)(2,1)}) %all-reduce.21.cloned.1.call-update) | async-done | bytes 131088 | tf_op jit(solution)/shard_map/psum | solution.py:9
  374.9 111.8 %all-reduce.35.cloned.1.call-done = (bf16[128,32,128]{2,0,1:T(8,128)(2,1)}, bf16[128,256]{1,0:T(8,128)(2,1)}) async-done(((bf16[128,32,128]{2,0,1:T(8,128)(2,1)}, bf16[128,256]{1,0:T(8,128)(2,1)}), (bf16[128,32,128]{2,0,1:T(8,128)(2,1)}, bf16[128,256]{1,0:T(8,128)(2,1)})) %all-reduce.35.cloned.1.call-update) | async-done | bytes 1114128 | tf_op jit(solution)/shard_map/psum | solution.py:9
  486.7 3.8 subtract_convert_fusion.1
  490.6 2.0 copy-done.3
  492.6 0.8 fusion.15
  493.5 0.0 all-reduce.25.cloned.1.call-start
  493.5 2.7 fusion.5
  496.2 0.2 fusion.8
  496.4 36.1 %all-reduce.23.cloned.1.call-done = bf16[4,128,128]{2,1,0:T(8,128)(2,1)} async-done(((bf16[4,128,128]{2,1,0:T(8,128)(2,1)}), bf16[4,128,128]{2,1,0:T(8,128)(2,1)}) %all-reduce.23.cloned.1.call-update) | async-done | bytes 131088 | tf_op jit(solution)/shard_map/psum | solution.py:9
  532.5 1.9 convolution_bitcast_fusion.3
  534.4 0.0 all-reduce.33.cloned.1.call-start
  534.5 0.8 fusion.22
  535.3 0.0 all-reduce.27.cloned.1.call-start
  535.4 0.7 broadcast_compare_fusion.2
  536.1 0.6 broadcast_compare_fusion.1
  536.7 103.3 %all-reduce.25.cloned.1.call-done = f32[128,256]{1,0:T(8,128)} async-done(((f32[128,256]{1,0:T(8,128)}), f32[128,256]{1,0:T(8,128)}) %all-reduce.25.cloned.1.call-update) | async-done | bytes 131088 | tf_op jit(solution)/shard_map/psum | solution.py:89
  639.9 109.0 %all-reduce.33.cloned.1.call-done = (bf16[128,32,128]{2,0,1:T(8,128)(2,1)}, bf16[128,256]{1,0:T(8,128)(2,1)}) async-done(((bf16[128,32,128]{2,0,1:T(8,128)(2,1)}, bf16[128,256]{1,0:T(8,128)(2,1)}), (bf16[128,32,128]{2,0,1:T(8,128)(2,1)}, bf16[128,256]{1,0:T(8,128)(2,1)})) %all-reduce.33.cloned.1.call-update) | async-done | bytes 1114128 | tf_op jit(solution)/shard_map/psum | solution.py:9
  749.0 1.1 bitcast_dynamic-update-slice_fusion.2
  750.0 0.9 convolution_bitcast_fusion.2
  751.0 0.0 all-reduce.29.cloned.1.call-start
  751.0 0.6 broadcast_compare_fusion
  751.6 101.7 %all-reduce.27.cloned.1.call-done = f32[128,256]{1,0:T(8,128)} async-done(((f32[128,256]{1,0:T(8,128)}), f32[128,256]{1,0:T(8,128)}) %all-reduce.27.cloned.1.call-update) | async-done | bytes 131088 | tf_op jit(solution)/shard_map/psum | solution.py:89
  853.3 1.1 bitcast_dynamic-update-slice_fusion.1
  854.3 0.9 convolution_bitcast_fusion.1
  855.3 0.2 all-reduce.31.cloned.1.call-start
  855.5 5.7 fusion.1
  861.3 96.5 %all-reduce.29.cloned.1.call-done = f32[128,256]{1,0:T(8,128)} async-done(((f32[128,256]{1,0:T(8,128)}), f32[128,256]{1,0:T(8,128)}) %all-reduce.29.cloned.1.call-update) | async-done | bytes 131088 | tf_op jit(solution)/shard_map/psum | solution.py:89
  957.7 1.1 bitcast_dynamic-update-slice_fusion
  958.8 0.9 convolution_bitcast_fusion
  959.8 0.9 fusion.10
  960.7 6.9 copy.30
  967.6 94.5 %all-reduce.31.cloned.1.call-done = f32[128,256]{1,0:T(8,128)} async-done(((f32[128,256]{1,0:T(8,128)}), f32[128,256]{1,0:T(8,128)}) %all-reduce.31.cloned.1.call-update) | async-done | bytes 131088 | tf_op jit(solution)/shard_map/psum | solution.py:89
  1062.1 1.0 fusion.24
  1063.1 0.7 copy-done.10
  (47 shorter events, 0.4 us)
Async XLA Ops:
  7.2 7.9 copy-start
  7.2 12.5 %copy-start.9 = (bf16[4,1,128,256]{3,2,1,0:T(8,128)(2,1)S(1)}, bf16[4,1,128,256]{3,2,1,0:T(8,128)(2,1)}, u32[]{:S(2)}) copy-start(bf16[4,1,128,256]{3,2,1,0:T(8,128)(2,1)} %param.8) | copy-start | bytes 786436
  7.2 16.3 %copy-start.15 = (s32[4,1,32,1]{2,3,1,0:T(1,128)S(1)}, s32[4,1,32,1]{2,3,1,0:T(1,128)}, u32[]{:S(2)}) copy-start(s32[4,1,32,1]{2,3,1,0:T(1,128)} %param.10) | copy-start | bytes 1540
  7.2 51.4 %all-reduce.17.cloned.1.call-start = ((), (), s32[]{:S(2)}) async-start(), calls=%async_computation | async-start | bytes 262144 | tf_op jit(solution)/shard_map/psum | solution.py:9
  15.9 154.7 %all-reduce.39.cloned.1.call-start = ((), (), s32[]{:S(2)}) async-start(), calls=%async_computation.11 | async-start | bytes 2228224 | tf_op jit(solution)/shard_map/psum | solution.py:9
  20.5 196.7 %all-reduce.19.cloned.1.call-start = ((), (), s32[]{:S(2)}) async-start(), calls=%async_computation.1 | async-start | bytes 262144 | tf_op jit(solution)/shard_map/psum | solution.py:9
  170.6 10.3 copy-start.7
  170.6 10.3 copy-start.11
  175.3 2.0 copy-start.2
  178.2 150.9 %all-reduce.37.cloned.1.call-start = ((), (), s32[]{:S(2)}) async-start(), calls=%async_computation.10 | async-start | bytes 2228224 | tf_op jit(solution)/shard_map/psum | solution.py:9
  182.0 192.9 %all-reduce.21.cloned.1.call-start = ((), (), s32[]{:S(2)}) async-start(), calls=%async_computation.2 | async-start | bytes 262144 | tf_op jit(solution)/shard_map/psum | solution.py:9
  329.1 9.5 copy-start.8
  329.1 9.5 copy-start.12
  333.0 2.0 copy-start.1
  335.8 150.9 %all-reduce.35.cloned.1.call-start = ((), (), s32[]{:S(2)}) async-start(), calls=%async_computation.9 | async-start | bytes 2228224 | tf_op jit(solution)/shard_map/psum | solution.py:9
  339.6 192.9 %all-reduce.23.cloned.1.call-start = ((), (), s32[]{:S(2)}) async-start(), calls=%async_computation.3 | async-start | bytes 262144 | tf_op jit(solution)/shard_map/psum | solution.py:9
  486.7 9.5 copy-start.4
  486.7 9.5 copy-start.13
  486.7 45.8 %copy-start.6 = (bf16[4,1,128,256]{3,2,1,0:T(8,128)(2,1)S(1)}, bf16[4,1,128,256]{3,2,1,0:T(8,128)(2,1)}, u32[]{:S(2)}) copy-start(bf16[4,1,128,256]{3,2,1,0:T(8,128)(2,1)} %param.9) | copy-start | bytes 786436
  490.6 2.0 copy-start.3
  493.5 146.5 %all-reduce.25.cloned.1.call-start = ((), (), s32[]{:S(2)}) async-start(), calls=%async_computation.4 | async-start | bytes 262144 | tf_op jit(solution)/shard_map/psum | solution.py:89
  532.5 323.0 %copy-start.5 = (bf16[4,128,128]{2,1,0:T(8,128)(2,1)S(1)}, bf16[4,128,128]{2,1,0:T(8,128)(2,1)}, u32[]{:S(2)}) copy-start(bf16[4,128,128]{2,1,0:T(8,128)(2,1)} %all-reduce.23.cloned.1.call-done) | copy-start | bytes 393220
  534.4 214.5 %all-reduce.33.cloned.1.call-start = ((), (), s32[]{:S(2)}) async-start(), calls=%async_computation.8 | async-start | bytes 2228224 | tf_op jit(solution)/shard_map/psum | solution.py:9
  535.3 318.0 %all-reduce.27.cloned.1.call-start = ((), (), s32[]{:S(2)}) async-start(), calls=%async_computation.5 | async-start | bytes 262144 | tf_op jit(solution)/shard_map/psum | solution.py:89
  751.0 206.8 %all-reduce.29.cloned.1.call-start = ((), (), s32[]{:S(2)}) async-start(), calls=%async_computation.6 | async-start | bytes 262144 | tf_op jit(solution)/shard_map/psum | solution.py:89
  855.3 206.8 %all-reduce.31.cloned.1.call-start = ((), (), s32[]{:S(2)}) async-start(), calls=%async_computation.7 | async-start | bytes 262144 | tf_op jit(solution)/shard_map/psum | solution.py:89
  855.5 104.2 %copy-start.14 = (bf16[128,256]{1,0:T(8,128)(2,1)S(1)}, bf16[128,256]{1,0:T(8,128)(2,1)}, u32[]{:S(2)}) copy-start(bf16[128,256]{1,0:T(8,128)(2,1)} %get-tuple-element.13) | copy-start | bytes 196612
  1063.1 0.7 copy-start.10
Sparse Core Ops, SparseCore 0:
  16.0 42.5 all-reduce.16
  62.7 107.9 all-reduce.38
  178.3 38.9 all-reduce.18
  221.1 107.9 all-reduce.36
  335.9 38.8 all-reduce.20
  378.8 107.9 all-reduce.34
  493.6 38.8 all-reduce.22
  536.3 103.5 all-reduce.24
  644.0 104.9 all-reduce.32
  752.6 100.6 all-reduce.26
  857.1 100.6 all-reduce.28
  961.4 100.6 all-reduce.30
where the time goes:
time: 1070 us
  waiting for transfers between devices  974 us (91%)
  matrix products  44.8 us (4%)
  between operations  29.6 us (3%)
  local copies, waits for them, and re-layouts  18 us (2%)
    psum x8, waiting for transfers between devices, spread(): return lax.psum(block, axis)  578 us
    psum x4, waiting for transfers between devices, body(): total = lax.psum(partial_sum, 'wide')  396 us
  transfers between devices with their start and end apart: 12, of which 12 were waited for; matrix products, arithmetic and copies ran while one was open for 3% of the time, Pallas kernels for 0%

commit v1 on v0

--- a/solution.py
+++ b/solution.py
@@ -86,7 +86,7 @@
         partial_sum = jnp.einsum(
             "rac,ran->cn", saved_left[section], current, preferred_element_type=jnp.float32
         )
-        total = lax.psum(partial_sum, "wide")
+        total = jnp.sum(lax.all_gather(partial_sum, "wide"), axis=0)
         corrected = (saved_pivot[section].astype(jnp.float32) - total).astype(jnp.bfloat16)
         result = jnp.einsum(
             "ac,cn->an", pivot_weight(target), corrected, preferred_element_type=jnp.float32

time: 1070 us -> 851 us (0.80)
  waiting for transfers between devices: 974 us -> 750 us
    psum x4 -> x0, waiting for transfers between devices: 396 us -> none  [body(): total = lax.psum(partial_sum, 'wide')]
    all_gather x0 -> x4, waiting for transfers between devices: none -> 173 us  [body(): total = jnp.sum(lax.all_gather(partial_sum, 'wide'), axis=0)]
where the time goes in v1:
time: 851 us; the launch traced here: 850 us
  waiting for transfers between devices  750 us (88%)
  matrix products  39.7 us (5%)
  between operations  30.3 us (4%)
  local copies, waits for them, and re-layouts  15.8 us (2%)
  other arithmetic  13.4 us (2%)
    psum x8, waiting for transfers between devices, spread(): return lax.psum(block, axis)  577 us
    all_gather x4, waiting for transfers between devices, body(): total = jnp.sum(lax.all_gather(partial_sum, 'wide'), axis=0)  173 us
  transfers between devices with their start and end apart: 12, of which 12 were waited for; matrix products, arithmetic and copies ran while one was open for 3% of the time, Pallas kernels for 0%

profile of v1, /device:TPU:1, one launch (start us, length us, event | category | flops | bytes accessed | tf_op | source)
XLA Modules:
  0.0 850.2 jit_solution(4111275735584590021)
XLA Ops:
  7.2 1.5 fusion.111
  12.6 0.8 select_reduce_fusion.1
  13.5 1.5 constant_dynamic-slice_fusion.1
  15.0 0.8 fusion.18
  16.0 1.3 constant_dynamic-slice_fusion
  17.3 0.7 select_reduce_fusion
  18.0 1.6 fusion.2
  19.7 0.8 fusion.19
  20.5 0.0 all-reduce.15.cloned.1.call-start
  24.7 33.9 %all-reduce.13.cloned.1.call-done = bf16[4,128,128]{2,1,0:T(8,128)(2,1)} async-done(((bf16[4,128,128]{2,1,0:T(8,128)(2,1)}), bf16[4,128,128]{2,1,0:T(8,128)(2,1)}) %all-reduce.13.cloned.1.call-update) | async-done | bytes 131088 | tf_op jit(solution)/shard_map/psum | solution.py:9
  58.6 112.0 %all-reduce.27.cloned.1.call-done = (bf16[128,32,128]{2,0,1:T(8,128)(2,1)}, bf16[128,256]{1,0:T(8,128)(2,1)}) async-done(((bf16[128,32,128]{2,0,1:T(8,128)(2,1)}, bf16[128,256]{1,0:T(8,128)(2,1)}), (bf16[128,32,128]{2,0,1:T(8,128)(2,1)}, bf16[128,256]{1,0:T(8,128)(2,1)})) %all-reduce.27.cloned.1.call-update) | async-done | bytes 1114128 | tf_op jit(solution)/shard_map/psum | solution.py:9
  170.6 4.7 fusion
  175.3 2.0 copy-done.2
  177.3 0.8 fusion.17
  178.2 0.0 all-reduce.25.cloned.1.call-start
  178.2 2.7 fusion.3
  180.9 0.2 fusion.6
  181.1 0.8 fusion.20
  185.9 31.3 %all-reduce.15.cloned.1.call-done = bf16[4,128,128]{2,1,0:T(8,128)(2,1)} async-done(((bf16[4,128,128]{2,1,0:T(8,128)(2,1)}), bf16[4,128,128]{2,1,0:T(8,128)(2,1)}) %all-reduce.15.cloned.1.call-update) | async-done | bytes 131088 | tf_op jit(solution)/shard_map/psum | solution.py:9
  217.2 111.8 %all-reduce.25.cloned.1.call-done = (bf16[128,32,128]{2,0,1:T(8,128)(2,1)}, bf16[128,256]{1,0:T(8,128)(2,1)}) async-done(((bf16[128,32,128]{2,0,1:T(8,128)(2,1)}, bf16[128,256]{1,0:T(8,128)(2,1)}), (bf16[128,32,128]{2,0,1:T(8,128)(2,1)}, bf16[128,256]{1,0:T(8,128)(2,1)})) %all-reduce.25.cloned.1.call-update) | async-done | bytes 1114128 | tf_op jit(solution)/shard_map/psum | solution.py:9
  329.1 3.8 subtract_convert_fusion.2
  332.9 2.0 copy-done.3
  334.9 0.8 fusion.16
  335.8 0.0 all-reduce.23.cloned.1.call-start
  335.8 2.7 fusion.4
  338.5 0.2 fusion.7
  338.8 0.8 fusion.21
  339.6 0.0 all-reduce.19.cloned.1.call-start
  343.5 31.4 %all-reduce.17.cloned.1.call-done = bf16[4,128,128]{2,1,0:T(8,128)(2,1)} async-done(((bf16[4,128,128]{2,1,0:T(8,128)(2,1)}), bf16[4,128,128]{2,1,0:T(8,128)(2,1)}) %all-reduce.17.cloned.1.call-update) | async-done | bytes 131088 | tf_op jit(solution)/shard_map/psum | solution.py:9
  374.9 111.8 %all-reduce.23.cloned.1.call-done = (bf16[128,32,128]{2,0,1:T(8,128)(2,1)}, bf16[128,256]{1,0:T(8,128)(2,1)}) async-done(((bf16[128,32,128]{2,0,1:T(8,128)(2,1)}, bf16[128,256]{1,0:T(8,128)(2,1)}), (bf16[128,32,128]{2,0,1:T(8,128)(2,1)}, bf16[128,256]{1,0:T(8,128)(2,1)})) %all-reduce.23.cloned.1.call-update) | async-done | bytes 1114128 | tf_op jit(solution)/shard_map/psum | solution.py:9
  486.7 3.8 subtract_convert_fusion.1
  490.6 2.0 copy-done.1
  492.6 0.8 fusion.15
  493.4 0.0 all-gather.9.cloned.1.call-start
  493.5 39.0 %all-reduce.19.cloned.1.call-done = bf16[4,128,128]{2,1,0:T(8,128)(2,1)} async-done(((bf16[4,128,128]{2,1,0:T(8,128)(2,1)}), bf16[4,128,128]{2,1,0:T(8,128)(2,1)}) %all-reduce.19.cloned.1.call-update) | async-done | bytes 131088 | tf_op jit(solution)/shard_map/psum | solution.py:9
  532.5 1.8 convolution_bitcast_fusion.3
  534.3 0.0 all-reduce.21.cloned.1.call-start
  534.4 0.2 fusion.8
  534.6 0.8 fusion.22
  535.5 2.7 fusion.5
  538.2 0.6 broadcast_compare_fusion.2
  538.9 45.5 %all-gather.9.cloned.1.call-done = f32[4096,256]{1,0:T(8,128)} async-done(((f32[128,256]{1,0:T(8,128)}), f32[4096,256]{1,0:T(8,128)}) %all-gather.9.cloned.1.call-update) | async-done | bytes 4194320 | tf_op jit(solution)/shard_map/all_gather | solution.py:89
  584.4 2.4 reduce_sum.36
  586.9 106.0 %all-reduce.21.cloned.1.call-done = (bf16[128,32,128]{2,0,1:T(8,128)(2,1)}, bf16[128,256]{1,0:T(8,128)(2,1)}) async-done(((bf16[128,32,128]{2,0,1:T(8,128)(2,1)}, bf16[128,256]{1,0:T(8,128)(2,1)}), (bf16[128,32,128]{2,0,1:T(8,128)(2,1)}, bf16[128,256]{1,0:T(8,128)(2,1)})) %all-reduce.21.cloned.1.call-update) | async-done | bytes 1114128 | tf_op jit(solution)/shard_map/psum | solution.py:9
  692.9 1.0 bitcast_dynamic-update-slice_fusion.2
  693.9 0.9 convolution_bitcast_fusion.2
  694.9 0.6 broadcast_compare_fusion.1
  695.5 46.2 %all-gather.11.cloned.1.call-done = f32[4096,256]{1,0:T(8,128)} async-done(((f32[128,256]{1,0:T(8,128)}), f32[4096,256]{1,0:T(8,128)}) %all-gather.11.cloned.1.call-update) | async-done | bytes 4194320 | tf_op jit(solution)/shard_map/all_gather | solution.py:89
  741.7 2.4 reduce_sum.37
  744.1 0.2 bitcast_dynamic-update-slice_fusion.1
  744.3 0.9 convolution_bitcast_fusion.1
  745.2 0.2 all-gather.15.cloned.1.call-start
  745.5 0.7 broadcast_compare_fusion
  746.2 44.7 %all-gather.13.cloned.1.call-done = f32[4096,256]{1,0:T(8,128)} async-done(((f32[128,256]{1,0:T(8,128)}), f32[4096,256]{1,0:T(8,128)}) %all-gather.13.cloned.1.call-update) | async-done | bytes 4194320 | tf_op jit(solution)/shard_map/all_gather | solution.py:89
  790.9 2.4 reduce_sum.38
  793.3 0.2 bitcast_dynamic-update-slice_fusion
  793.5 0.9 convolution_bitcast_fusion
  794.4 3.4 fusion.1
  797.9 4.7 copy.38
  802.6 0.9 fusion.10
  803.5 36.5 %all-gather.15.cloned.1.call-done = f32[4096,256]{1,0:T(8,128)} async-done(((f32[128,256]{1,0:T(8,128)}), f32[4096,256]{1,0:T(8,128)}) %all-gather.15.cloned.1.call-update) | async-done | bytes 4194320 | tf_op jit(solution)/shard_map/all_gather | solution.py:89
  840.0 2.4 reduce_sum.39
  842.5 0.1 fusion.24
  842.6 0.7 copy-done.11
  (53 shorter events, 0.5 us)
Async XLA Ops:
  7.2 7.8 copy-start
  7.2 12.5 %copy-start.10 = (bf16[4,1,128,256]{3,2,1,0:T(8,128)(2,1)S(1)}, bf16[4,1,128,256]{3,2,1,0:T(8,128)(2,1)}, u32[]{:S(2)}) copy-start(bf16[4,1,128,256]{3,2,1,0:T(8,128)(2,1)} %param.8) | copy-start | bytes 786436
  7.2 16.8 %copy-start.16 = (s32[4,1,32,1]{2,3,1,0:T(1,128)S(1)}, s32[4,1,32,1]{2,3,1,0:T(1,128)}, u32[]{:S(2)}) copy-start(s32[4,1,32,1]{2,3,1,0:T(1,128)} %param.10) | copy-start | bytes 1540
  7.2 51.4 %all-reduce.13.cloned.1.call-start = ((), (), s32[]{:S(2)}) async-start(), calls=%async_computation | async-start | bytes 262144 | tf_op jit(solution)/shard_map/psum | solution.py:9
  15.9 154.7 %all-reduce.27.cloned.1.call-start = ((), (), s32[]{:S(2)}) async-start(), calls=%async_computation.11 | async-start | bytes 2228224 | tf_op jit(solution)/shard_map/psum | solution.py:9
  20.5 196.7 %all-reduce.15.cloned.1.call-start = ((), (), s32[]{:S(2)}) async-start(), calls=%async_computation.1 | async-start | bytes 262144 | tf_op jit(solution)/shard_map/psum | solution.py:9
  170.6 10.3 %copy-start.8 = (bf16[4,128,128]{2,1,0:T(8,128)(2,1)S(1)}, bf16[4,128,128]{2,1,0:T(8,128)(2,1)}, u32[]{:S(2)}) copy-start(bf16[4,128,128]{2,1,0:T(8,128)(2,1)} %all-reduce.13.cloned.1.call-done) | copy-start | bytes 393220
  170.6 10.3 %copy-start.12 = (bf16[128,256]{1,0:T(8,128)(2,1)S(1)}, bf16[128,256]{1,0:T(8,128)(2,1)}, u32[]{:S(2)}) copy-start(bf16[128,256]{1,0:T(8,128)(2,1)} %get-tuple-element.19) | copy-start | bytes 196612
  175.3 2.0 copy-start.2
  178.2 150.9 %all-reduce.25.cloned.1.call-start = ((), (), s32[]{:S(2)}) async-start(), calls=%async_computation.10 | async-start | bytes 2228224 | tf_op jit(solution)/shard_map/psum | solution.py:9
  182.0 192.9 %all-reduce.17.cloned.1.call-start = ((), (), s32[]{:S(2)}) async-start(), calls=%async_computation.2 | async-start | bytes 262144 | tf_op jit(solution)/shard_map/psum | solution.py:9
  329.1 9.5 %copy-start.9 = (bf16[4,128,128]{2,1,0:T(8,128)(2,1)S(1)}, bf16[4,128,128]{2,1,0:T(8,128)(2,1)}, u32[]{:S(2)}) copy-start(bf16[4,128,128]{2,1,0:T(8,128)(2,1)} %all-reduce.15.cloned.1.call-done) | copy-start | bytes 393220
  329.1 9.5 %copy-start.13 = (bf16[128,256]{1,0:T(8,128)(2,1)S(1)}, bf16[128,256]{1,0:T(8,128)(2,1)}, u32[]{:S(2)}) copy-start(bf16[128,256]{1,0:T(8,128)(2,1)} %get-tuple-element.17) | copy-start | bytes 196612
  332.9 2.0 copy-start.3
  335.8 150.9 %all-reduce.23.cloned.1.call-start = ((), (), s32[]{:S(2)}) async-start(), calls=%async_computation.9 | async-start | bytes 2228224 | tf_op jit(solution)/shard_map/psum | solution.py:9
  339.6 192.9 %all-reduce.19.cloned.1.call-start = ((), (), s32[]{:S(2)}) async-start(), calls=%async_computation.3 | async-start | bytes 262144 | tf_op jit(solution)/shard_map/psum | solution.py:9
  486.7 45.8 %copy-start.6 = (bf16[4,1,128,256]{3,2,1,0:T(8,128)(2,1)S(1)}, bf16[4,1,128,256]{3,2,1,0:T(8,128)(2,1)}, u32[]{:S(2)}) copy-start(bf16[4,1,128,256]{3,2,1,0:T(8,128)(2,1)} %param.9) | copy-start | bytes 786436
  486.7 47.7 %copy-start.4 = (bf16[4,128,128]{2,1,0:T(8,128)(2,1)S(1)}, bf16[4,128,128]{2,1,0:T(8,128)(2,1)}, u32[]{:S(2)}) copy-start(bf16[4,128,128]{2,1,0:T(8,128)(2,1)} %all-reduce.17.cloned.1.call-done) | copy-start | bytes 393220
  486.7 47.7 %copy-start.14 = (bf16[128,256]{1,0:T(8,128)(2,1)S(1)}, bf16[128,256]{1,0:T(8,128)(2,1)}, u32[]{:S(2)}) copy-start(bf16[128,256]{1,0:T(8,128)(2,1)} %get-tuple-element.15) | copy-start | bytes 196612
  490.6 2.0 copy-start.1
  493.4 91.0 %all-gather.9.cloned.1.call-start = ((), (), s32[]{:S(2)}) async-start(), calls=%async_computation.4 | async-start | bytes 4325376 | tf_op jit(solution)/shard_map/all_gather | solution.py:89
  534.3 158.5 %all-reduce.21.cloned.1.call-start = ((), (), s32[]{:S(2)}) async-start(), calls=%async_computation.8 | async-start | bytes 2228224 | tf_op jit(solution)/shard_map/psum | solution.py:9
  538.2 203.5 %all-gather.11.cloned.1.call-start = ((), (), s32[]{:S(2)}) async-start(), calls=%async_computation.5 | async-start | bytes 4325376 | tf_op jit(solution)/shard_map/all_gather | solution.py:89
  694.8 96.1 %all-gather.13.cloned.1.call-start = ((), (), s32[]{:S(2)}) async-start(), calls=%async_computation.6 | async-start | bytes 4325376 | tf_op jit(solution)/shard_map/all_gather | solution.py:89
  744.1 50.3 %copy-start.5 = (bf16[4,128,128]{2,1,0:T(8,128)(2,1)S(1)}, bf16[4,128,128]{2,1,0:T(8,128)(2,1)}, u32[]{:S(2)}) copy-start(bf16[4,128,128]{2,1,0:T(8,128)(2,1)} %all-reduce.19.cloned.1.call-done) | copy-start | bytes 393220
  744.1 50.3 %copy-start.7 = (bf16[128,32,128]{2,0,1:T(8,128)(2,1)S(1)}, bf16[128,32,128]{2,0,1:T(8,128)(2,1)}, u32[]{:S(2)}) copy-start(bf16[128,32,128]{2,0,1:T(8,128)(2,1)} %get-tuple-element.12) | copy-start | bytes 3145732
  745.2 94.8 %all-gather.15.cloned.1.call-start = ((), (), s32[]{:S(2)}) async-start(), calls=%async_computation.7 | async-start | bytes 4325376 | tf_op jit(solution)/shard_map/all_gather | solution.py:89
  797.9 4.7 copy-start.15
  842.6 0.7 copy-start.11
Sparse Core Ops, SparseCore 0:
  16.0 42.5 all-reduce.12
  62.6 107.9 all-reduce.26
  178.3 38.9 all-reduce.14
  221.1 107.9 all-reduce.24
  335.9 38.8 all-reduce.16
  378.7 107.9 all-reduce.22
  493.6 38.8 all-reduce.18
  535.3 49.0 all-gather.8
  588.4 104.3 all-reduce.20
  695.5 46.1 all-gather.10
  745.4 45.4 all-gather.12
  794.5 45.4 all-gather.14
